TPU v7x, 32 devices: a whole 2x2x4 slice. The times are simulated.
32 devices in a mesh: grp: 2 (over y), wide: 4 (over z), freq: 2 (over x), pol: 2 (over core).
Axes of the slice: x: 2, y: 2, z: 4, core: 2. Of those that a mesh axis runs over, the one named last changes fastest.
Arguments:
- visibilities: float32 [2, 4096, 8, 384], P(None, ('grp', 'wide'), 'freq', 'pol'), parts along dimension 1, may hold values from -6 to 6
- beams: bfloat16 [8, 8, 2, 384, 768], P('wide', 'freq', None, 'pol'), may hold values from -0.21875 to 0.21875
- spectra: float32 [8, 5, 768], P('freq'), may hold values from 0.1 to 1
- m_orders: int32 [8], replicated, may hold values from 0 to 1023, as said below
Outputs:
- msdata: float32 [16, 8, 2, 384], P(('grp', 'wide'), 'freq', None, 'pol'), parts along dimension 0
- weighted: float32 [16, 8, 2, 384], P(('grp', 'wide'), 'freq', None, 'pol'), parts along dimension 0
There are 2 independent parts, one for each index of `grp`. A program takes and returns all parts, laid end to end along the dimension named above; an argument that names none is the same for every part. Nothing has to cross between parts.
Inputs may be any that keep to these rules, and one draw needn't show every extreme that they name: `m_orders`: the m-orders are distinct, and 0 and 1023 are always among them.
All inputs are finite; a program needn't handle non-finite values.
Results may differ from a plain program's by a relative error of at most 0.0039.
Values sent between devices are 32-bit elements; how exact they have to be, the bound alone decides.
A program may use at most 64 MiB of HBM per device.

v0:
```python
import math
import jax
import jax.numpy as jnp
from jax import lax
from jax.sharding import PartitionSpec as P

TIME = 2048
BAND = 4


def shifted(array, axis, by):
    size = lax.axis_size(axis)
    return lax.ppermute(array, axis, [(i, (i + by) % size) for i in range(size)])


def fourier_tables(orders, times):
    product = orders[:, None] * times[None, :] % TIME
    angle = product.astype(jnp.float32) * (2.0 * math.pi / TIME)
    factor = 1.0 / math.sqrt(TIME)
    return (jnp.cos(angle) * factor, jnp.sin(angle) * factor)


def transform(orders, times, block):
    cosine, sine_tab = fourier_tables(orders, times)
    count = times.shape[0]
    data_real = block[0].reshape(count, -1)
    data_imag = block[1].reshape(count, -1)
    exact_mode = lax.Precision.HIGHEST
    part_real = jnp.dot(
        cosine, data_real, precision=exact_mode, preferred_element_type=jnp.float32
    ) + jnp.dot(sine_tab, data_imag, precision=exact_mode, preferred_element_type=jnp.float32)
    part_imag = jnp.dot(
        cosine, data_imag, precision=exact_mode, preferred_element_type=jnp.float32
    ) - jnp.dot(sine_tab, data_real, precision=exact_mode, preferred_element_type=jnp.float32)
    shape_out = (orders.shape[0], block.shape[2], block.shape[3])
    return jnp.stack([part_real.reshape(shape_out), part_imag.reshape(shape_out)], axis=2)


def shards(visibilities, beams, spectra, m_orders):
    local_blocks = beams.shape[1]
    local_times = visibilities.shape[1]
    first_time = lax.axis_index("wide") * local_times
    times = first_time + jnp.arange(local_times, dtype=jnp.int32)
    msdata = lax.psum_scatter(
        transform(m_orders, times, visibilities), "wide", scatter_dimension=0, tiled=True
    )
    rounded = msdata.astype(jnp.bfloat16)
    round_real = rounded[:, :, 0]
    round_imag = rounded[:, :, 1]
    stacked = jnp.stack(
        [jnp.stack([round_real, round_imag], 2), jnp.stack([round_imag, -round_real], 2)], 2
    )
    partial_proj = lax.dot_general(
        stacked, beams, (((3, 4), (2, 3)), ((0, 1), (0, 1))), preferred_element_type=jnp.float32
    )
    projected = lax.psum(partial_proj, "pol")
    following = shifted(projected, "freq", -1)
    extended = jnp.concatenate([projected, following], axis=1)
    mixed = spectra[None, :, 0, None, :] * projected
    for offset in range(1, BAND + 1):
        mixed = (
            mixed + spectra[None, :, offset, None, :] * extended[:, offset : offset + local_blocks]
        )
    coupled = mixed.astype(jnp.bfloat16)
    cop_real = coupled[:, :, 0]
    cop_imag = coupled[:, :, 1]
    paired = jnp.stack([jnp.stack([cop_real, -cop_imag], 2), jnp.stack([cop_imag, cop_real], 2)], 2)
    weighted = lax.dot_general(
        paired, beams, (((3, 4), (2, 4)), ((0, 1), (0, 1))), preferred_element_type=jnp.float32
    )
    return (msdata, weighted)


def solution(mesh):
    return jax.shard_map(
        shards,
        mesh=mesh,
        in_specs=(
            P(None, ("grp", "wide"), "freq", "pol"),
            P("wide", "freq", None, "pol", None),
            P("freq", None, None),
            P(),
        ),
        out_specs=(
            P(("grp", "wide"), "freq", None, "pol"),
            P(("grp", "wide"), "freq", None, "pol"),
        ),
        check_vma=False,
    )
```

profile of v0, /device:TPU:0, one launch (start us, length us, event | category | flops | bytes accessed | tf_op | source)
XLA Modules:
  0.0 47.3 jit_solution(1263961565827750037)
XLA Ops:
  0.6 0.0 copy-start.1
  0.7 2.2 %fusion.44 = (f32[1,512,4,192]{1,3,2,0:T(8,128)S(1)}, f32[1,512,4,192]{1,3,2,0:T(8,128)S(1)}) fusion(f32[2,512,4,192]{1,3,2,0:T(8,128)} %param.4), kind=kLoop, calls=%fused_computation.70 | loop fusion | bytes 6291456 | tf_op jit(solution)/shard_map/slice | solution.py:26
  2.9 0.0 copy-done.1
  2.9 1.4 %fusion.13 = f32[8,768]{1,0:T(8,128)S(1)} fusion(f32[512,768]{0,1:T(8,128)S(1)} %bitcast.34, s32[512]{0:T(512)S(1)} %iota_add_fusion, s32[8]{0:T(128)S(1)} %copy-done.1), kind=kOutput, calls=%fused_computation.31 | convolution fusion | flops 37810176 | bytes 1599520 | tf_op jit(solution)/shard_map/dot_general | solution.py:29
  4.3 1.5 %fusion.12 = f32[8,768]{1,0:T(8,128)S(1)} fusion(f32[512,768]{0,1:T(8,128)S(1)} %bitcast.36, s32[512]{0:T(512)S(1)} %iota_add_fusion, s32[8]{0:T(128)S(1)} %copy-done.1), kind=kOutput, calls=%fused_computation.30 | convolution fusion | flops 37810176 | bytes 1599520 | tf_op jit(solution)/shard_map/dot_general | solution.py:32
  5.8 1.5 %convolution_add_fusion = f32[8,768]{1,0:T(8,128)S(1)} fusion(f32[8,768]{1,0:T(8,128)S(1)} %fusion.13, f32[512,768]{0,1:T(8,128)S(1)} %bitcast.37, s32[512]{0:T(512)S(1)} %iota_add_fusion, s32[8]{0:T(128)S(1)} %copy-done.1), kind=kOutput, calls=%fused_computation.2 | convolution fusion | flops 37816320 | bytes 1624096 | tf_op jit(solution)/shard_map/dot_general | solution.py:31
  7.3 0.1 stack_reshape.6
  7.4 1.4 %convolution_subtract_fusion = f32[8,768]{1,0:T(8,128)S(1)} fusion(f32[8,768]{1,0:T(8,128)S(1)} %fusion.12, f32[512,768]{0,1:T(8,128)S(1)} %bitcast.35, s32[512]{0:T(512)S(1)} %iota_add_fusion, s32[8]{0:T(128)S(1)} %copy-done.1), kind=kOutput, calls=%fused_computation.1 | convolution fusion | flops 37816320 | bytes 1624096 | tf_op jit(solution)/shard_map/dot_general | solution.py:34
  8.8 0.1 stack_reshape.7
  9.0 21.5 %all-reduce = f32[8,4,2,192]{3,1,2,0:T(4,128)S(1)} all-reduce(f32[8,4,2,192]{3,1,2,0:T(4,128)S(1)} %pad_maximum_fusion), channel_id=2, replica_groups=mesh['grp'=2,'wide'=4,'freq'=2,'pol'=2] {'wide'}, use_global_device_ids=true, to_apply=%region_0.1.clone | all-reduce | flops 12288 | bytes 98304
  30.5 0.0 copy-done.2
  30.5 0.6 %dynamic-slice = u32[1]{0:T(128)} dynamic-slice(u32[32]{0:T(128)S(1)} %copy-done.2, u32[]{:T(128)S(6)} %add.44), dynamic_slice_sizes={1} | dynamic-slice | bytes 12
  31.9 0.0 copy-start
  31.9 3.1 %convolution_bitcast_fusion = f32[2,4,2,768]{3,2,1,0:T(2,128)S(1)} fusion(bf16[2,4,2,192,768]{4,3,2,1,0:T(8,128)(2,1)} %param.5, bf16[2,4,1,2,192]{4,2,3,1,0:T(2,128)(2,1)S(1)} %copy.24, bf16[2,4,1,2,192]{4,2,3,1,0:T(2,128)(2,1)S(1)} %copy.23), kind=kOutput, calls=%fused_computation | convolution fusion | flops 9461760 | bytes 4780032 | tf_op jit(solution)/shard_map/dot_general | solution.py:53
  35.0 3.5 %psum.7 = f32[2,4,2,768]{3,2,1,0:T(2,128)S(1)} all-reduce(f32[2,4,2,768]{3,2,1,0:T(2,128)S(1)} %convolution_bitcast_fusion), channel_id=1, replica_groups=mesh['grp'=2,'wide'=4,'freq'=2,'pol'=2] {'pol'}, use_global_device_ids=true, to_apply=%region_1.2 | all-reduce | flops 12288 | bytes 98304 | tf_op jit(solution)/shard_map/psum | solution.py:56
  38.5 1.6 %collective-permute-start = (f32[2,4,2,768]{3,2,1,0:T(2,128)S(1)}, f32[2,4,2,768]{3,2,1,0:T(2,128)S(1)}, u32[]{:S(2)}, u32[]{:S(2)}) collective-permute-start(f32[2,4,2,768]{3,2,1,0:T(2,128)S(1)} %psum.7), channel_id=1, source_target_pairs={{0,2},{2,0},{1,3},{3,1},{4,6},{6,4},{5,7},{7,5},{8,10},{10,8},{9,1... | collective-permute-start | bytes 147464 | tf_op jit(solution)/shard_map/ppermute | solution.py:13
  40.1 0.0 copy-done
  40.1 0.6 %copy.26 = f32[2,4,2,192]{3,2,1,0:T(2,128)} copy(f32[2,4,2,192]{3,1,2,0:T(4,128)S(1)} %get-tuple-element.5) | data formatting | bytes 24576
  40.7 2.0 %collective-permute-done = f32[2,4,2,768]{3,2,1,0:T(2,128)S(1)} collective-permute-done((f32[2,4,2,768]{3,2,1,0:T(2,128)S(1)}, f32[2,4,2,768]{3,2,1,0:T(2,128)S(1)}, u32[]{:S(2)}, u32[]{:S(2)}) %collective-permute-start) | collective-permute-done | bytes 49184 | tf_op jit(solution)/shard_map/ppermute | solution.py:13
  42.7 0.1 fusion.5
  42.8 0.1 slice_negate_fusion.1
  42.9 0.1 maximum_bitcast_fusion
  43.0 0.1 pad_maximum_fusion.1
  43.1 4.3 %convolution_bitcast_fusion.1 = f32[2,4,2,192]{3,2,1,0:T(2,128)} fusion(bf16[2,4,2,192,768]{4,3,2,1,0:T(8,128)(2,1)} %param.5, bf16[2,4,2,2,768]{4,3,1,0,2:T(2,128)(2,1)S(1)} %pad_maximum_fusion.1), kind=kOutput, calls=%fused_computation.3 | convolution fusion | flops 9437184 | bytes 4780032 | tf_op jit(solution)/shard_map/dot_general | solution.py:68
  (11 shorter events, 0.1 us)
Async XLA Ops:
  0.6 2.2 %copy-start.1 = (s32[8]{0:T(128)S(1)}, s32[8]{0:T(128)}, u32[]{:S(2)}) copy-start(s32[8]{0:T(128)} %param.7) | copy-start | bytes 100
  5.8 24.7 %copy-start.2 = (u32[32]{0:T(128)S(1)}, u32[32]{0:T(128)}, u32[]{:S(2)}) copy-start(u32[32]{0:T(128)} %constant.29) | copy-start | bytes 388
  31.9 8.2 %copy-start = (f32[4,5,768]{2,0,1:T(4,128)S(1)}, f32[4,5,768]{2,0,1:T(4,128)}, u32[]{:S(2)}) copy-start(f32[4,5,768]{2,0,1:T(4,128)} %param.6) | copy-start | bytes 184324
  38.5 4.2 %collective-permute-start = (f32[2,4,2,768]{3,2,1,0:T(2,128)S(1)}, f32[2,4,2,768]{3,2,1,0:T(2,128)S(1)}, u32[]{:S(2)}, u32[]{:S(2)}) collective-permute-start(f32[2,4,2,768]{3,2,1,0:T(2,128)S(1)} %psum.7), channel_id=1, source_target_pairs={{0,2},{2,0},{1,3},{3,1},{4,6},{6,4},{5,7},{7,5},{8,10},{10,8},{9,1... | collective-permute-start | bytes 147464 | tf_op jit(solution)/shard_map/ppermute | solution.py:13
where the time goes:
time: 47.6 us; the launch traced here: 47.3 us
  blocking collectives  25 us (53%)
  matrix products  13.3 us (28%)
  local copies, waits for them, and re-layouts  3.68 us (8%)
  waiting for transfers between devices  1.96 us (4%)
  starting transfers between devices  1.56 us (3%)
  between operations  1.46 us (3%)
    unnamed x1, blocking collectives  21.5 us
    dot_general x1, matrix products, shards(): lax.dot_general(paired, beams, (((3, 4), (2, 4)), ((0, 1), (0, 1))), pref...  4.27 us
    psum x1, blocking collectives, shards(): projected = lax.psum(partial_proj, 'pol')  3.52 us
    dot_general x1, matrix products, shards(): lax.dot_general(stacked, beams, (((3, 4), (2, 3)), ((0, 1), (0, 1))), pre...  3.14 us
    slice x1, local copies, waits for them, and re-layouts, transform(): data_real = block[0].reshape(count, -1)  2.19 us
    ppermute x1, waiting for transfers between devices, shifted(): lax.ppermute(array, axis, [(i, (i + by) % size) for i in range(size)])  1.96 us
    ppermute x1, starting transfers between devices, shifted(): lax.ppermute(array, axis, [(i, (i + by) % size) for i in range(size)])  1.56 us
    dot_general x1, matrix products, transform(): jnp.dot(cosine, data_imag, precision=exact_mode, preferred_element_type=j...  1.48 us
  transfers between devices with their start and end apart: 1, of which 1 were waited for; matrix products, arithmetic and copies ran while one was open for 1% of the time, Pallas kernels for 0%

commit v1 on v0

--- a/solution.py
+++ b/solution.py
@@ -53,7 +53,7 @@
     partial_proj = lax.dot_general(
         stacked, beams, (((3, 4), (2, 3)), ((0, 1), (0, 1))), preferred_element_type=jnp.float32
     )
-    projected = lax.psum(partial_proj, "pol")
+    projected = jnp.sum(lax.all_gather(partial_proj, "pol"), axis=0)
     following = shifted(projected, "freq", -1)
     extended = jnp.concatenate([projected, following], axis=1)
     mixed = spectra[None, :, 0, None, :] * projected

time: 47.6 us -> 45.9 us (0.964)
  blocking collectives: 25 us -> 23.4 us
    psum x1 -> x0, blocking collectives: 3.52 us -> none  [shards(): projected = lax.psum(partial_proj, 'pol')]
    all_gather x0 -> x1, blocking collectives: none -> 1.88 us  [shards(): projected = jnp.sum(lax.all_gather(partial_proj, 'pol'), axis=0)]
    unnamed x9 -> x8, local copies, waits for them, and re-layouts: 1.22 us -> 1.22 us
where the time goes in v1:
time: 45.9 us; the launch traced here: 45.6 us
  blocking collectives  23.4 us (51%)
  matrix products  13.3 us (29%)
  local copies, waits for them, and re-layouts  3.75 us (8%)
  waiting for transfers between devices  1.97 us (4%)
  starting transfers between devices  1.56 us (3%)
  between operations  1.46 us (3%)
    unnamed x1, blocking collectives  21.5 us
    dot_general x1, matrix products, shards(): lax.dot_general(paired, beams, (((3, 4), (2, 4)), ((0, 1), (0, 1))), pref...  4.29 us
    dot_general x1, matrix products, shards(): lax.dot_general(stacked, beams, (((3, 4), (2, 3)), ((0, 1), (0, 1))), pre...  3.14 us
    slice x1, local copies, waits for them, and re-layouts, transform(): data_real = block[0].reshape(count, -1)  2.19 us
    ppermute x1, waiting for transfers between devices, shifted(): lax.ppermute(array, axis, [(i, (i + by) % size) for i in range(size)])  1.97 us
    all_gather x1, blocking collectives, shards(): projected = jnp.sum(lax.all_gather(partial_proj, 'pol'), axis=0)  1.88 us
    ppermute x1, starting transfers between devices, shifted(): lax.ppermute(array, axis, [(i, (i + by) % size) for i in range(size)])  1.56 us
    dot_general x1, matrix products, transform(): jnp.dot(cosine, data_imag, precision=exact_mode, preferred_element_type=j...  1.48 us
  transfers between devices with their start and end apart: 1, of which 1 were waited for; matrix products, arithmetic and copies ran while one was open for 1% of the time, Pallas kernels for 0%

profile of v1, /device:TPU:0, one launch (start us, length us, event | category | flops | bytes accessed | tf_op | source)
XLA Modules:
  0.0 45.6 jit_solution(14485958154055186723)
XLA Ops:
  0.6 0.0 copy-start.1
  0.7 2.2 %fusion.52 = (f32[1,512,4,192]{1,3,2,0:T(8,128)S(1)}, f32[1,512,4,192]{1,3,2,0:T(8,128)S(1)}) fusion(f32[2,512,4,192]{1,3,2,0:T(8,128)} %param.4), kind=kLoop, calls=%fused_computation.77 | loop fusion | bytes 6291456 | tf_op jit(solution)/shard_map/slice | solution.py:26
  2.9 0.0 copy-done.1
  2.9 1.4 %fusion.20 = f32[8,768]{1,0:T(8,128)S(1)} fusion(f32[512,768]{0,1:T(8,128)S(1)} %bitcast.35, s32[512]{0:T(512)S(1)} %iota_add_fusion, s32[8]{0:T(128)S(1)} %copy-done.1), kind=kOutput, calls=%fused_computation.39 | convolution fusion | flops 37810176 | bytes 1599520 | tf_op jit(solution)/shard_map/dot_general | solution.py:29
  4.3 1.5 %fusion.19 = f32[8,768]{1,0:T(8,128)S(1)} fusion(f32[512,768]{0,1:T(8,128)S(1)} %bitcast.37, s32[512]{0:T(512)S(1)} %iota_add_fusion, s32[8]{0:T(128)S(1)} %copy-done.1), kind=kOutput, calls=%fused_computation.38 | convolution fusion | flops 37810176 | bytes 1599520 | tf_op jit(solution)/shard_map/dot_general | solution.py:32
  5.8 0.0 copy-start.2
  5.8 1.5 %convolution_add_fusion = f32[8,768]{1,0:T(8,128)S(1)} fusion(f32[8,768]{1,0:T(8,128)S(1)} %fusion.20, f32[512,768]{0,1:T(8,128)S(1)} %bitcast.38, s32[512]{0:T(512)S(1)} %iota_add_fusion, s32[8]{0:T(128)S(1)} %copy-done.1), kind=kOutput, calls=%fused_computation.2 | convolution fusion | flops 37816320 | bytes 1624096 | tf_op jit(solution)/shard_map/dot_general | solution.py:31
  7.3 0.1 stack_reshape.6
  7.4 1.4 %convolution_subtract_fusion = f32[8,768]{1,0:T(8,128)S(1)} fusion(f32[8,768]{1,0:T(8,128)S(1)} %fusion.19, f32[512,768]{0,1:T(8,128)S(1)} %bitcast.36, s32[512]{0:T(512)S(1)} %iota_add_fusion, s32[8]{0:T(128)S(1)} %copy-done.1), kind=kOutput, calls=%fused_computation.1 | convolution fusion | flops 37816320 | bytes 1624096 | tf_op jit(solution)/shard_map/dot_general | solution.py:34
  8.8 0.1 stack_reshape.7
  9.0 21.5 %all-reduce = f32[8,4,2,192]{3,1,2,0:T(4,128)S(1)} all-reduce(f32[8,4,2,192]{3,1,2,0:T(4,128)S(1)} %pad_maximum_fusion), channel_id=3, replica_groups=mesh['grp'=2,'wide'=4,'freq'=2,'pol'=2] {'wide'}, use_global_device_ids=true, to_apply=%region_0.1.clone | all-reduce | flops 12288 | bytes 98304
  30.5 0.0 copy-done.2
  30.5 0.6 %dynamic-slice = u32[1]{0:T(128)} dynamic-slice(u32[32]{0:T(128)S(1)} %copy-done.2, u32[]{:T(128)S(6)} %add.42), dynamic_slice_sizes={1} | dynamic-slice | bytes 12
  31.9 0.0 copy-start
  31.9 3.1 %convolution_bitcast_fusion = f32[2,4,2,768]{3,2,1,0:T(2,128)S(1)} fusion(bf16[2,4,2,192,768]{4,3,2,1,0:T(8,128)(2,1)} %param.5, bf16[2,4,1,2,192]{4,2,3,1,0:T(2,128)(2,1)S(1)} %copy.35, bf16[2,4,1,2,192]{4,2,3,1,0:T(2,128)(2,1)S(1)} %copy.34), kind=kOutput, calls=%fused_computation | convolution fusion | flops 9461760 | bytes 4780032 | tf_op jit(solution)/shard_map/dot_general | solution.py:53
  35.0 1.9 %all-gather = f32[4,4,2,768]{3,1,2,0:T(4,128)S(1)} all-gather(f32[2,4,2,768]{3,1,2,0:T(4,128)S(1)} %copy.36), channel_id=2, replica_groups=mesh['grp'=2,'wide'=4,'freq'=2,'pol'=2] {'pol'}, dimensions={0}, use_global_device_ids=true | all-gather | bytes 147456 | tf_op jit(solution)/shard_map/all_gather | solution.py:56
  36.9 1.6 %collective-permute-start = (f32[2,4,2,768]{3,1,2,0:T(4,128)S(1)}, f32[2,4,2,768]{3,1,2,0:T(4,128)S(1)}, u32[]{:S(2)}, u32[]{:S(2)}) collective-permute-start(f32[2,4,2,768]{3,1,2,0:T(4,128)S(1)} %reduce_sum.9), channel_id=1, source_target_pairs={{0,2},{2,0},{1,3},{3,1},{4,6},{6,4},{5,7},{7,5},{8,10},{10,8},{9,1... | collective-permute-start | bytes 147464 | tf_op jit(solution)/shard_map/ppermute | solution.py:13
  38.5 0.0 copy-done
  38.5 0.6 %copy.41 = f32[2,4,2,192]{3,2,1,0:T(2,128)} copy(f32[2,4,2,192]{3,1,2,0:T(4,128)S(1)} %get-tuple-element.7) | data formatting | bytes 24576
  39.1 2.0 %collective-permute-done = f32[2,4,2,768]{3,1,2,0:T(4,128)S(1)} collective-permute-done((f32[2,4,2,768]{3,1,2,0:T(4,128)S(1)}, f32[2,4,2,768]{3,1,2,0:T(4,128)S(1)}, u32[]{:S(2)}, u32[]{:S(2)}) %collective-permute-start) | collective-permute-done | bytes 49184 | tf_op jit(solution)/shard_map/ppermute | solution.py:13
  41.1 0.1 fusion.12
  41.3 4.3 %convolution_bitcast_fusion.1 = f32[2,4,2,192]{3,2,1,0:T(2,128)} fusion(bf16[2,4,2,192,768]{4,3,2,1,0:T(8,128)(2,1)} %param.5, bf16[2,4,1,2,768]{4,2,3,1,0:T(2,128)(2,1)S(1)} %copy.40, bf16[2,4,1,2,768]{4,2,3,1,0:T(2,128)(2,1)S(1)} %copy.39), kind=kOutput, calls=%fused_computation.3 | convolution fusion | flops 9535488 | bytes 4780032 | tf_op jit(solution)/shard_map/dot_general | solution.py:68
  (14 shorter events, 0.3 us)
Async XLA Ops:
  0.6 2.2 %copy-start.1 = (s32[8]{0:T(128)S(1)}, s32[8]{0:T(128)}, u32[]{:S(2)}) copy-start(s32[8]{0:T(128)} %param.7) | copy-start | bytes 100
  5.8 24.7 %copy-start.2 = (u32[32]{0:T(128)S(1)}, u32[32]{0:T(128)}, u32[]{:S(2)}) copy-start(u32[32]{0:T(128)} %constant.31) | copy-start | bytes 388
  31.9 6.6 %copy-start = (f32[4,5,768]{2,0,1:T(4,128)S(1)}, f32[4,5,768]{2,0,1:T(4,128)}, u32[]{:S(2)}) copy-start(f32[4,5,768]{2,0,1:T(4,128)} %param.6) | copy-start | bytes 184324
  36.9 4.2 %collective-permute-start = (f32[2,4,2,768]{3,1,2,0:T(4,128)S(1)}, f32[2,4,2,768]{3,1,2,0:T(4,128)S(1)}, u32[]{:S(2)}, u32[]{:S(2)}) collective-permute-start(f32[2,4,2,768]{3,1,2,0:T(4,128)S(1)} %reduce_sum.9), channel_id=1, source_target_pairs={{0,2},{2,0},{1,3},{3,1},{4,6},{6,4},{5,7},{7,5},{8,10},{10,8},{9,1... | collective-permute-start | bytes 147464 | tf_op jit(solution)/shard_map/ppermute | solution.py:13
